TPU v7x, 256 devices: a whole 4x4x8 slice. The times are simulated.
256 devices in a mesh: buf: 32 (over x, y, core), lat: 8 (over z).
Axes of the slice: x: 4, y: 4, z: 8, core: 2. Of those that a mesh axis runs over, the one named last changes fastest.
Arguments:
- buffer: bfloat16 [8192, 4096], P('buf'), may hold values from -6 to 6
- sample_rows: int32 [8192], P('lat'), may hold values from 0 to 8191, as said below
- window: bfloat16 [24576, 4096], P('buf'), may hold values from -6 to 6
- enc_scale: float32 [8192], P('lat'), may hold values from 0.5 to 2
- dec_bias: float32 [4096], replicated, may hold values from -3 to 3
Outputs:
- recon: bfloat16 [24576, 4096], P('buf', 'lat')
Inputs may be any that keep to these rules, and one draw needn't show every extreme that they name: `sample_rows`: entry k names the buffer row sampled for reseeded latent k; shard s of the buffer holds rows s * 256 to (s + 1) * 256 - 1. In each aligned block of 32 entries at most 2 name rows of one shard, and in every block some shard gives exactly 2. In each owner's 1024 entries at most 64 name rows of one shard, and some shard gives exactly 64.
All inputs are finite; a program needn't handle non-finite values.
Results may differ from a plain program's by a relative error of at most 0.018.
Values may be sent and summed in bfloat16 or wider, within the bound.
A program may use at most 128 MiB of HBM per device.

v0:
```python
import jax
import jax.numpy as jnp
from jax import lax
from jax.sharding import PartitionSpec as P


def unit_rows(picked_rows):
    values = picked_rows.astype(jnp.float32)
    squares = jnp.sum(values * values, axis=1, keepdims=True)
    return (values * lax.rsqrt(squares + 1e-06)).astype(jnp.bfloat16)


def encode_block(centered, unit_block, scale_block):
    scores = lax.dot_general(
        centered, unit_block, (((1,), (1,)), ((), ())), preferred_element_type=jnp.float32
    )
    return jnp.maximum(scores * scale_block[None, :], 0.0).astype(jnp.bfloat16)


def pick_units(buffer, pick_index):
    picked = jnp.take(buffer, jnp.maximum(pick_index, 0), axis=0)
    picked = jnp.where((pick_index >= 0)[:, None], picked, jnp.zeros_like(picked))
    return unit_rows(picked)


def on_device(buffer, sample_rows, window, enc_scale, dec_bias):
    shard_count = lax.axis_size("buf")
    shard_index = lax.axis_index("buf")
    owner_count = sample_rows.shape[0]
    slot_count = owner_count // shard_count
    shard_rows = buffer.shape[0]
    capacity = 2 + (slot_count - 1) // shard_count
    source = sample_rows // shard_rows
    offset = sample_rows - source * shard_rows
    centered = (window.astype(jnp.float32) - dec_bias[None, :]).astype(jnp.bfloat16)
    positions = jnp.arange(owner_count, dtype=jnp.int32)
    own_capacity = shard_count * capacity
    matching = source[:, None] == source[None, :]
    earlier = positions[:, None] < positions[None, :]
    owner_rank = jnp.sum((matching & earlier).astype(jnp.int32), axis=0)
    room_iota = jnp.arange(own_capacity, dtype=jnp.int32)
    chosen = (source == shard_index)[:, None] & (owner_rank[:, None] == room_iota[None, :])
    pick_index = jnp.sum(jnp.where(chosen, offset[:, None] + 1, 0), axis=0) - 1
    packed = pick_units(buffer, pick_index)
    collected = lax.all_gather(packed, "buf", axis=0, tiled=True)
    all_units = jnp.take(collected, source * own_capacity + owner_rank, axis=0)
    active_all = encode_block(centered, all_units, enc_scale)
    partial_value = jnp.dot(active_all, all_units, preferred_element_type=jnp.float32)
    rounded = partial_value.astype(jnp.bfloat16).astype(jnp.float32)
    summed = lax.psum_scatter(
        rounded.astype(jnp.bfloat16), "lat", scatter_dimension=1, tiled=True
    ).astype(jnp.float32)
    feature_count = summed.shape[1]
    bias_part = lax.dynamic_slice_in_dim(
        dec_bias, lax.axis_index("lat") * feature_count, feature_count
    )
    return (summed + bias_part[None, :]).astype(jnp.bfloat16)


def solution(mesh):
    in_specs = (P("buf", None), P("lat"), P("buf", None), P("lat"), P())
    out_specs = P("buf", "lat")
    return jax.shard_map(
        on_device, mesh=mesh, in_specs=in_specs, out_specs=out_specs, check_vma=False
    )
```

profile of v0, /device:TPU:1, one launch (start us, length us, event | category | flops | bytes accessed | tf_op | source)
XLA Modules:
  0.0 220.5 jit_solution(11854953599494018754)
XLA Ops:
  6.5 0.0 copy-start
  6.5 0.0 all-gather.2.cloned.1.call-start
  6.5 0.8 add_select_fusion
  7.4 0.4 convert_reduce_fusion
  7.8 0.7 broadcast_clamp_fusion
  8.5 0.7 compare_and_fusion
  9.2 0.2 select_reduce_fusion
  9.4 0.0 copy-done
  9.4 0.9 gather_fusion
  10.3 0.3 fusion.3
  10.6 1.0 fusion.4
  11.7 0.0 all-gather.2.cloned.1.call-update
  11.7 0.0 reduce-scatter.2.cloned.1.call-start
  11.7 81.8 %all-gather.2.cloned.1.call-done = bf16[2048,4096]{1,0:T(8,128)(2,1)} async-done(((bf16[64,4096]{1,0:T(8,128)(2,1)}), bf16[2048,4096]{1,0:T(8,128)(2,1)}) %all-gather.2.cloned.1.call-update) | async-done | bytes 16777232 | tf_op jit(solution)/shard_map/all_gather | solution.py:45
  93.6 0.0 copy-start.2
  93.6 0.0 copy-start.3
  93.6 23.0 %gather_fusion.1 = bf16[1024,4096]{1,0:T(8,128)(2,1)} fusion(bf16[2048,4096]{1,0:T(8,128)(2,1)} %all-gather.2.cloned.1.call-done, s32[1024]{0:T(1024)S(1)} %get-tuple-element.7), kind=kCustom, calls=%fused_computation.1 | custom fusion | bytes 16781312 | tf_op jit(solution)/shard_map/jit(_take)/gather | solution.py:46
  116.6 0.0 copy-done.2
  116.6 0.0 copy-done.3
  116.6 0.0 copy-start.1
  116.6 11.6 %maximum_convert_fusion = bf16[768,1024]{1,0:T(8,128)(2,1)S(1)} fusion(bf16[1024,4096]{1,0:T(8,128)(2,1)} %gather_fusion.1, pred[1024]{0:T(1024)(128)(4,1)S(1)} %get-tuple-element.5, bf16[768,4096]{1,0:T(8,128)(2,1)} %param.7, f32[4096]{0:T(1024)S(1)} %copy-done.2, f32[1024]{0:T(1024)S(1)} %copy-done.3), kind=kOutput, calls=%fused_computation.10 | convolution fusion | flops 6458441728 | bytes 16274432 | tf_op jit(solution)/shard_map/dot_general | solution.py:14
  128.3 0.0 copy-done.1
  128.3 8.8 %convolution_convert_fusion = bf16[768,4096]{1,0:T(8,128)(2,1)} fusion(bf16[768,1024]{1,0:T(8,128)(2,1)S(1)} %maximum_convert_fusion, bf16[1024,4096]{1,0:T(8,128)(2,1)S(1)} %copy-done.1, pred[1024]{0:T(1024)(128)(4,1)S(1)} %get-tuple-element.5), kind=kOutput, calls=%fused_computation.4 | convolution fusion | flops 6449790976 | bytes 16253952 | tf_op jit(solution)/shard_map/dot_general | solution.py:48
  137.1 0.0 reduce-scatter.2.cloned.1.call-update
  137.1 0.1 dynamic_slice.3
  137.2 74.4 %reduce-scatter.2.cloned.1.call-done = bf16[768,512]{1,0:T(8,128)(2,1)} async-done(((bf16[768,4096]{1,0:T(8,128)(2,1)}), bf16[768,512]{1,0:T(8,128)(2,1)}) %reduce-scatter.2.cloned.1.call-update) | async-done | bytes 786448 | tf_op jit(solution)/shard_map/reduce_scatter | solution.py:50
  211.5 2.2 add_convert_fusion
  (4 shorter events, 0.0 us)
Async XLA Ops:
  6.5 2.9 %copy-start = (bf16[256,4096]{1,0:T(8,128)(2,1)S(1)}, bf16[256,4096]{1,0:T(8,128)(2,1)}, u32[]{:S(2)}) copy-start(bf16[256,4096]{1,0:T(8,128)(2,1)} %param.5) | copy-start | bytes 6291460
  6.5 87.0 %all-gather.2.cloned.1.call-start = ((), (), s32[]{:S(2)}) async-start(), calls=%async_computation.1 | async-start | bytes 17301504 | tf_op jit(solution)/shard_map/all_gather | solution.py:45
  11.7 199.9 %reduce-scatter.2.cloned.1.call-start = ((), (), s32[]{:S(2)}) async-start(), calls=%async_computation.2 | async-start | bytes 7077888 | tf_op jit(solution)/shard_map/reduce_scatter | solution.py:50
  93.6 23.0 %copy-start.2 = (f32[4096]{0:T(1024)S(1)}, f32[4096]{0:T(1024)}, u32[]{:S(2)}) copy-start(f32[4096]{0:T(1024)} %param.9) | copy-start | bytes 49156
  93.6 23.0 %copy-start.3 = (f32[1024]{0:T(1024)S(1)}, f32[1024]{0:T(1024)}, u32[]{:S(2)}) copy-start(f32[1024]{0:T(1024)} %param.8) | copy-start | bytes 12292
  116.6 11.7 %copy-start.1 = (bf16[1024,4096]{1,0:T(8,128)(2,1)S(1)}, bf16[1024,4096]{1,0:T(8,128)(2,1)}, u32[]{:S(2)}) copy-start(bf16[1024,4096]{1,0:T(8,128)(2,1)} %gather_fusion.1) | copy-start | bytes 25165828
Sparse Core Ops, SparseCore 0:
  11.8 81.7 all-gather.1
  137.2 74.2 reduce-scatter.1
where the time goes:
time: 221 us
  waiting for transfers between devices  156 us (71%)
  local copies, waits for them, and re-layouts  24 us (11%)
  matrix products  20.4 us (9%)
  between operations  13.5 us (6%)
  other arithmetic  6.37 us (3%)
    all_gather x1, waiting for transfers between devices, on_device(): collected = lax.all_gather(packed, 'buf', axis=0, tiled=True)  81.8 us
    reduce_scatter x1, waiting for transfers between devices, on_device(): lax.psum_scatter(rounded.astype(jnp.bfloat16), 'lat', scatter_dimension=1...  74.4 us
    gather x1, local copies, waits for them, and re-layouts, on_device(): all_units = jnp.take(collected, source * own_capacity + owner_rank, axis=0)  23 us
    dot_general x1, matrix products, encode_block(): lax.dot_general(centered, unit_block, (((1,), (1,)), ((), ())), preferred...  11.6 us
    dot_general x1, matrix products, on_device(): jnp.dot(active_all, all_units, preferred_element_type=jnp.float32)  8.79 us
  transfers between devices with their start and end apart: 2, of which 2 were waited for; matrix products, arithmetic and copies ran while one was open for 0% of the time, Pallas kernels for 0%

commit v1 on v0

--- a/solution.py
+++ b/solution.py
@@ -42,7 +42,9 @@
     chosen = (source == shard_index)[:, None] & (owner_rank[:, None] == room_iota[None, :])
     pick_index = jnp.sum(jnp.where(chosen, offset[:, None] + 1, 0), axis=0) - 1
     packed = pick_units(buffer, pick_index)
-    collected = lax.all_gather(packed, "buf", axis=0, tiled=True)
+    collected = jnp.concatenate(
+        lax.all_to_all(jnp.stack([packed] * lax.axis_size("buf")), "buf", 0, 0), axis=0
+    )
     all_units = jnp.take(collected, source * own_capacity + owner_rank, axis=0)
     active_all = encode_block(centered, all_units, enc_scale)
     partial_value = jnp.dot(active_all, all_units, preferred_element_type=jnp.float32)

time: 221 us -> 334 us (1.51)
  blocking collectives: 0 us -> 194 us
  waiting for transfers between devices: 156 us -> 74.4 us
    all_to_all x0 -> x1, blocking collectives: none -> 194 us  [on_device(): lax.all_to_all(jnp.stack([packed] * lax.axis_size('buf')), 'buf', 0, 0)]
    all_gather x1 -> x0, waiting for transfers between devices: 81.8 us -> none  [on_device(): collected = lax.all_gather(packed, 'buf', axis=0, tiled=True)]
  transfers between devices with their start and end apart: 2 -> 1, of which waited for: 2 -> 1; matrix products, arithmetic and copies ran while one was open for 0% -> 0% of each run, Pallas kernels for 0% -> 0%
where the time goes in v1:
time: 334 us
  blocking collectives  194 us (58%)
  waiting for transfers between devices  74.4 us (22%)
  local copies, waits for them, and re-layouts  25.9 us (8%)
  matrix products  20.4 us (6%)
  between operations  13.5 us (4%)
  other arithmetic  5.58 us (2%)
    all_to_all x1, blocking collectives, on_device(): lax.all_to_all(jnp.stack([packed] * lax.axis_size('buf')), 'buf', 0, 0)  194 us
    reduce_scatter x1, waiting for transfers between devices, on_device(): lax.psum_scatter(rounded.astype(jnp.bfloat16), 'lat', scatter_dimension=1...  74.4 us
    gather x1, local copies, waits for them, and re-layouts, on_device(): all_units = jnp.take(collected, source * own_capacity + owner_rank, axis=0)  23 us
    dot_general x1, matrix products, encode_block(): lax.dot_general(centered, unit_block, (((1,), (1,)), ((), ())), preferred...  11.7 us
    dot_general x1, matrix products, on_device(): jnp.dot(active_all, all_units, preferred_element_type=jnp.float32)  8.79 us
  transfers between devices with their start and end apart: 1, of which 1 were waited for; matrix products, arithmetic and copies ran while one was open for 0% of the time, Pallas kernels for 0%

profile of v1, /device:TPU:1, one launch (start us, length us, event | category | flops | bytes accessed | tf_op | source)
XLA Modules:
  0.0 333.8 jit_solution(16674362965533190082)
XLA Ops:
  6.5 0.0 copy-start
  6.5 0.0 reduce-scatter.2.cloned.1.call-start
  6.5 0.8 add_select_fusion
  7.4 0.4 convert_reduce_fusion
  7.8 0.7 broadcast_clamp_fusion
  8.5 0.7 compare_and_fusion
  9.2 0.2 select_reduce_fusion
  9.4 0.0 copy-done
  9.4 0.9 gather_fusion
  10.3 0.4 fusion.3
  10.6 0.2 fusion.4
  10.9 2.0 stack.2
  12.9 193.9 %all_to_all.5 = bf16[32,64,4096]{2,1,0:T(8,128)(2,1)} all-to-all(bf16[32,64,4096]{2,1,0:T(8,128)(2,1)S(1)} %stack.2), channel_id=1, replica_groups=mesh['buf'=32,'lat'=8] {'buf'}, dimensions={0} | all-to-all | bytes 33554432 | tf_op jit(solution)/shard_map/all_to_all | solution.py:46
  206.8 0.0 copy-start.2
  206.8 0.0 copy-start.3
  206.8 23.0 %gather_fusion.1 = bf16[1024,4096]{1,0:T(8,128)(2,1)} fusion(bf16[2048,4096]{1,0:T(8,128)(2,1)} %bitcast.2, s32[1024]{0:T(1024)S(1)} %get-tuple-element.7), kind=kCustom, calls=%fused_computation.1 | custom fusion | bytes 16781312 | tf_op jit(solution)/shard_map/jit(_take)/gather | solution.py:48
  229.8 0.0 copy-done.2
  229.8 0.0 copy-done.3
  229.8 0.0 copy-start.1
  229.8 11.7 %maximum_convert_fusion = bf16[768,1024]{1,0:T(8,128)(2,1)S(1)} fusion(bf16[1024,4096]{1,0:T(8,128)(2,1)} %gather_fusion.1, pred[1024]{0:T(1024)(128)(4,1)S(1)} %get-tuple-element.5, bf16[768,4096]{1,0:T(8,128)(2,1)} %param.7, f32[4096]{0:T(1024)S(1)} %copy-done.2, f32[1024]{0:T(1024)S(1)} %copy-done.3), kind=kOutput, calls=%fused_computation.10 | convolution fusion | flops 6458441728 | bytes 16274432 | tf_op jit(solution)/shard_map/dot_general | solution.py:14
  241.5 0.0 copy-done.1
  241.5 8.8 %convolution_convert_fusion = bf16[768,4096]{1,0:T(8,128)(2,1)} fusion(bf16[768,1024]{1,0:T(8,128)(2,1)S(1)} %maximum_convert_fusion, bf16[1024,4096]{1,0:T(8,128)(2,1)S(1)} %copy-done.1, pred[1024]{0:T(1024)(128)(4,1)S(1)} %get-tuple-element.5), kind=kOutput, calls=%fused_computation.4 | convolution fusion | flops 6449790976 | bytes 16253952 | tf_op jit(solution)/shard_map/dot_general | solution.py:50
  250.3 0.0 reduce-scatter.2.cloned.1.call-update
  250.3 0.1 dynamic_slice.3
  250.4 74.4 %reduce-scatter.2.cloned.1.call-done = bf16[768,512]{1,0:T(8,128)(2,1)} async-done(((bf16[768,4096]{1,0:T(8,128)(2,1)}), bf16[768,512]{1,0:T(8,128)(2,1)}) %reduce-scatter.2.cloned.1.call-update) | async-done | bytes 786448 | tf_op jit(solution)/shard_map/reduce_scatter | solution.py:52
  324.8 2.2 add_convert_fusion
  (4 shorter events, 0.0 us)
Async XLA Ops:
  6.5 2.9 copy-start
  6.5 318.2 %reduce-scatter.2.cloned.1.call-start = ((), (), s32[]{:S(2)}) async-start(), calls=%async_computation.2 | async-start | bytes 7077888 | tf_op jit(solution)/shard_map/reduce_scatter | solution.py:52
  206.8 23.0 %copy-start.2 = (f32[4096]{0:T(1024)S(1)}, f32[4096]{0:T(1024)}, u32[]{:S(2)}) copy-start(f32[4096]{0:T(1024)} %param.9) | copy-start | bytes 49156
  206.8 23.0 %copy-start.3 = (f32[1024]{0:T(1024)S(1)}, f32[1024]{0:T(1024)}, u32[]{:S(2)}) copy-start(f32[1024]{0:T(1024)} %param.8) | copy-start | bytes 12292
  229.8 11.7 %copy-start.1 = (bf16[1024,4096]{1,0:T(8,128)(2,1)S(1)}, bf16[1024,4096]{1,0:T(8,128)(2,1)}, u32[]{:S(2)}) copy-start(bf16[1024,4096]{1,0:T(8,128)(2,1)} %gather_fusion.1) | copy-start | bytes 25165828
Sparse Core Ops, SparseCore 0:
  250.4 74.2 reduce-scatter.1
